TPU v7x, 32 devices: a whole 2x2x4 slice. The times are simulated.
32 devices in a mesh: grp: 2 (over x), yz: 8 (over z, y), gx: 2 (over core).
Axes of the slice: x: 2, y: 2, z: 4, core: 2. Of those that a mesh axis runs over, the one named last changes fastest.
Arguments:
- field: bfloat16 [4096, 256, 128], P(('grp', 'gx'), 'yz'), parts along dimension 0, may hold values from -6 to 6
- sketch_seeds: int32 [12], P('grp'), parts along dimension 0, may hold values from 1 to 32748
Outputs:
- basis: float32 [4096, 256], P(('grp', 'gx')), parts along dimension 0
- core: bfloat16 [512, 256, 128], P(('grp', 'gx'), 'yz'), parts along dimension 0
There are 2 independent parts, one for each index of `grp`. A program takes and returns all parts, laid end to end along the dimension named above; each array names one. Nothing has to cross between parts.
All inputs are finite; a program needn't handle non-finite values.
Results may differ from a plain program's by a relative error of at most 0.0057.
Values sent between devices are 32-bit elements; how exact they have to be, the bound alone decides.
No kernel may reach another device: no remote copies, remote signals or barrier semaphores. Data moves between devices by JAX's collectives and lax.ppermute only.
A program may use at most 64 MiB of HBM per device.

v0:
```python
import math
import jax
import jax.numpy as jnp
from jax import lax
from jax.sharding import PartitionSpec as P

RANK = 256
prime = 32749


def omega_table(seeds, start, count):
    place = (start + jnp.arange(count, dtype=jnp.int32) + 1)[:, None]
    column = (jnp.arange(RANK, dtype=jnp.int32) + 1)[None, :]
    first = seeds[0] * place % prime
    second = (seeds[1] * column + seeds[2]) % prime
    square = place * place % prime
    third = seeds[2] * column % prime
    mixed = (first * second % prime + square * third % prime) % prime
    return mixed.astype(jnp.float32) * (2.0 / prime) - 1.0


def local(field, sketch_seeds):
    x_local, y_local, z_local = field.shape
    y_start = lax.axis_index("yz") * y_local
    omega_z = omega_table(sketch_seeds[3:6], 0, z_local).astype(jnp.bfloat16)
    omega_y = omega_table(sketch_seeds[0:3], y_start, y_local)
    block = math.gcd(y_local, 8)

    def add_block(total, index):
        rows = lax.dynamic_slice_in_dim(field, index * block, block, 1)
        proj = jnp.dot(
            rows.reshape(x_local * block, z_local), omega_z, preferred_element_type=jnp.float32
        ).reshape(x_local, block, RANK)
        weight_y = lax.dynamic_slice_in_dim(omega_y, index * block, block, 0)
        return (total + jnp.sum(proj * weight_y[None], axis=1), None)

    partial_value, unused = lax.scan(
        add_block,
        jnp.zeros((x_local, RANK), jnp.float32),
        jnp.arange(y_local // block, dtype=jnp.int32),
    )
    sketch = lax.psum(partial_value, "yz")
    gram = lax.psum(
        jnp.dot(
            sketch.T, sketch, precision=lax.Precision.HIGHEST, preferred_element_type=jnp.float32
        ),
        "gx",
    )
    lower = jnp.linalg.cholesky(gram)
    basis = lax.linalg.triangular_solve(
        lower, sketch, left_side=False, lower=True, transpose_a=True
    )
    basis_half = basis.astype(jnp.bfloat16)
    flat = field.reshape(x_local, y_local * z_local)
    owned_rank = RANK // lax.axis_size("gx")
    core = lax.psum_scatter(
        lax.dot_general(
            basis_half, flat, (((0,), (0,)), ((), ())), preferred_element_type=jnp.float32
        ),
        "gx",
        scatter_dimension=0,
        tiled=True,
    )
    return (basis, core.reshape(owned_rank, y_local, z_local).astype(jnp.bfloat16))


def solution(mesh):
    in_specs = (P(("grp", "gx"), "yz", None), P("grp"))
    out_specs = (P(("grp", "gx"), None), P(("grp", "gx"), "yz", None))
    return jax.shard_map(local, mesh=mesh, in_specs=in_specs, out_specs=out_specs, check_vma=False)
```

profile of v0, /device:TPU:0, one launch (start us, length us, event | category | flops | bytes accessed | tf_op | source)
XLA Modules:
  0.0 233.7 jit_solution(5224184737601147460)
XLA Ops:
  7.2 1.6 fusion.53
  12.8 20.5 %while.13 = (s32[]{:T(128)}, f32[1024,256]{1,0:T(8,128)S(1)}, s32[4]{0:T(128)S(1)}, bf16[1024,32,128]{2,1,0:T(8,128)(2,1)}, f32[32,256]{1,0:T(8,128)S(1)}, /*ind...) while((s32[]{:T(128)}, f32[1024,256]{1,0:T(8,128)S(1)}, ...), condition=%wide.region_2.3_spmd.clone, body=%wide.region_0.2_spmd.clone.sunk | while | flops 542146560 | bytes 10513617 | solution.py:37
  14.1 1.7 constant_dynamic-slice_fusion.8
  15.9 1.7 multiply_reduce_fusion.2
  19.3 1.7 constant_dynamic-slice_fusion.8
  21.0 1.7 multiply_reduce_fusion.2
  24.4 1.7 constant_dynamic-slice_fusion.8
  26.1 1.7 multiply_reduce_fusion.2
  29.5 1.7 constant_dynamic-slice_fusion.8
  31.3 1.7 multiply_reduce_fusion.2
  34.3 81.1 %all-reduce.4.cloned.1.call-done = f32[1024,256]{1,0:T(8,128)} async-done(((f32[1024,256]{1,0:T(8,128)}), f32[1024,256]{1,0:T(8,128)}) %all-reduce.4.cloned.1.call-update) | async-done | bytes 1048592 | tf_op jit(solution)/shard_map/psum | solution.py:42
  115.4 4.1 %fusion.54 = f32[256,256]{0,1:T(8,128)} fusion(f32[1024,256]{1,0:T(8,128)} %all-reduce.4.cloned.1.call-done), kind=kOutput, calls=%fused_computation.98 | convolution fusion | flops 805306368 | bytes 1310720 | tf_op jit(solution)/shard_map/dot_general | solution.py:44
  119.8 17.7 %all-reduce.6.cloned.1.call-done = f32[256,256]{0,1:T(8,128)} async-done(((f32[256,256]{0,1:T(8,128)}), f32[256,256]{0,1:T(8,128)}) %all-reduce.6.cloned.1.call-update) | async-done | bytes 262160 | tf_op jit(solution)/shard_map/psum | solution.py:43
  139.6 11.7 %cholesky.50 = f32[128,128]{1,0:T(8,128)S(1)} custom-call(f32[128,128]{1,0:T(8,128)S(1)} %cholesky.118), custom_call_target="Cholesky" | custom-call | tf_op jit(solution)/shard_map/jit(cholesky)/cholesky | solution.py:49
  152.0 9.8 %custom-call.14 = f32[1,128,128]{1,2,0:T(8,128)S(1)} custom-call(f32[1,128,128]{2,1,0:T(8,128)S(1)} %get-tuple-element.121), custom_call_target="InvertDiagBlocksLowerTriangular" | custom-call | tf_op jit(solution)/shard_map/jit(cholesky)/cholesky | solution.py:49
  162.4 11.7 %cholesky.105 = f32[128,128]{1,0:T(8,128)S(1)} custom-call(f32[128,128]{1,0:T(8,128)S(1)} %convolution_subtract_fusion.1), custom_call_target="Cholesky" | custom-call | tf_op jit(solution)/shard_map/jit(cholesky)/cholesky | solution.py:49
  176.3 4.3 %while.12 = (s32[]{:T(128)}, f32[256,256]{1,0:T(8,128)S(1)}, s32[2,2]{1,0:T(2,128)S(1)}, f32[2,128,128]{2,1,0:T(8,128)S(1)}, s32[]{:T(128)}) while((s32[]{:T(128)}, f32[256,256]{1,0:T(8,128)S(1)}, s32[2,2]{1,0:T(2,128)S(1)}, f32[2,128,128]{2,1,0:T(8,128)S(1)}, s32[]{:T(128)}) %tuple.57), condition=%wide.while_cond, body=%wide.while_body.sunk | while | flops 2 | bytes 131189 | solution.py:50
  177.1 1.4 bitcast_dynamic-update-slice_fusion.2
  179.1 1.4 bitcast_dynamic-update-slice_fusion.2
  180.5 19.7 %custom-call.15 = f32[2,128,128]{1,2,0:T(8,128)S(1)} custom-call(f32[2,128,128]{2,1,0:T(8,128)S(1)} %get-tuple-element.42), custom_call_target="InvertDiagBlocksLowerTriangular" | custom-call | tf_op jit(solution)/shard_map/triangular_solve | solution.py:50
  202.5 8.3 %fusion.29 = f32[256,4096]{1,0:T(8,128)} fusion(bf16[128,8,32,128]{3,2,1,0:T(8,128)(2,1)} %bitcast.54, f32[1024,128]{0,1:T(8,128)S(1)} %fusion.36, f32[1024,128]{0,1:T(8,128)S(1)} %fusion.32), kind=kOutput, calls=%fused_computation.38 | convolution fusion | flops 2148532224 | bytes 13631488 | tf_op jit(solution)/shard_map/dot_general | solution.py:57
  210.9 1.3 copy.7
  212.2 12.0 %reduce-scatter.2.cloned.1.call-done = f32[128,4096]{1,0:T(8,128)} async-done(((f32[256,4096]{1,0:T(8,128)}), f32[128,4096]{1,0:T(8,128)}) %reduce-scatter.2.cloned.1.call-update) | async-done | bytes 2097168 | tf_op jit(solution)/shard_map/reduce_scatter | solution.py:56
  224.2 1.8 convert_bitcast_fusion
  (52 shorter events, 17.9 us)
Async XLA Ops:
  7.2 108.2 %all-reduce.4.cloned.1.call-start = ((), (), s32[]{:S(2)}) async-start(), calls=%async_computation.1 | async-start | bytes 2097152 | tf_op jit(solution)/shard_map/psum | solution.py:42
  33.3 1.0 copy-start
  34.3 103.3 %all-reduce.6.cloned.1.call-start = ((), (), s32[]{:S(2)}) async-start(), calls=%async_computation.2 | async-start | bytes 524288 | tf_op jit(solution)/shard_map/psum | solution.py:43
  115.4 84.8 %copy-start.1 = (f32[1024,256]{1,0:T(8,128)S(1)}, f32[1024,256]{1,0:T(8,128)}, u32[]{:S(2)}) copy-start(f32[1024,256]{1,0:T(8,128)} %all-reduce.4.cloned.1.call-done) | copy-start | bytes 3145732
  119.6 104.6 %reduce-scatter.2.cloned.1.call-start = ((), (), s32[]{:S(2)}) async-start(), calls=%async_computation.3 | async-start | bytes 6291456 | tf_op jit(solution)/shard_map/reduce_scatter | solution.py:56
Sparse Core Ops, SparseCore 0:
  34.4 80.9 all-reduce.3
  119.7 17.8 all-reduce.5
  210.9 13.2 reduce-scatter.1
where the time goes:
time: 234 us
  waiting for transfers between devices  111 us (47%)
  other arithmetic  62.3 us (27%)
  matrix products  21.9 us (9%)
  local copies, waits for them, and re-layouts  19.9 us (9%)
  between operations  15.3 us (7%)
  loops' own time  3.19 us (1%)
    psum x1, waiting for transfers between devices, local(): sketch = lax.psum(partial_value, 'yz')  81.1 us
    another operation x7, other arithmetic, local(): lower = jnp.linalg.cholesky(gram)  34.7 us
    another operation x4, other arithmetic, local(): lax.linalg.triangular_solve(lower, sketch, left_side=False, lower=True, t...  19.8 us
    psum x1, waiting for transfers between devices, local(): lax.psum(jnp.dot(sketch.T, sketch, precision=lax.Precision.HIGHEST, prefe...  17.7 us
    reduce_scatter x1, waiting for transfers between devices, local(): lax.psum_scatter(lax.dot_general(basis_half, flat, (((0,), (0,)), ((), ()...  12 us
    dot_general x1, matrix products, local(): lax.dot_general(basis_half, flat, (((0,), (0,)), ((), ())), preferred_ele...  8.29 us
    dynamic_slice x4, local copies, waits for them, and re-layouts, add_block(): rows = lax.dynamic_slice_in_dim(field, index * block, block, 1)  6.93 us
    dot_general x4, matrix products, add_block(): jnp.dot(rows.reshape(x_local * block, z_local), omega_z, preferred_elemen...  6.81 us
  transfers between devices with their start and end apart: 3, of which 3 were waited for; matrix products, arithmetic and copies ran while one was open for 1% of the time, Pallas kernels for 0%

commit v1 on v0

--- a/solution.py
+++ b/solution.py
@@ -3,6 +3,7 @@
 import jax.numpy as jnp
 from jax import lax
 from jax.sharding import PartitionSpec as P
+from jax.lax import axis_size, ppermute
 
 RANK = 256
 prime = 32749
@@ -20,6 +21,14 @@
 
 
 def local(field, sketch_seeds):
+
+    def balance_roads(row_data):
+        high = row_data
+        count_all = axis_size("yz")
+        for rr in [i0 for i0 in (1, 2, 4, 8, 16) if i0 < count_all]:
+            high = high + ppermute(high, "yz", tuple(((kk, kk ^ rr) for kk in range(count_all))))
+        return high
+
     x_local, y_local, z_local = field.shape
     y_start = lax.axis_index("yz") * y_local
     omega_z = omega_table(sketch_seeds[3:6], 0, z_local).astype(jnp.bfloat16)
@@ -39,7 +48,7 @@
         jnp.zeros((x_local, RANK), jnp.float32),
         jnp.arange(y_local // block, dtype=jnp.int32),
     )
-    sketch = lax.psum(partial_value, "yz")
+    sketch = balance_roads(partial_value)
     gram = lax.psum(
         jnp.dot(
             sketch.T, sketch, precision=lax.Precision.HIGHEST, preferred_element_type=jnp.float32

time: 234 us -> 250 us (1.068)
  waiting for transfers between devices: 111 us -> 121 us
  starting transfers between devices: 0.3 us -> 7.62 us
    ppermute x0 -> x3, waiting for transfers between devices: none -> 90.2 us  [balance_roads(): ppermute(high, 'yz', tuple(((kk, kk ^ rr) for kk in range(count_all))))]
    psum x1 -> x0, waiting for transfers between devices: 81.1 us -> none  [local(): sketch = lax.psum(partial_value, 'yz')]
    ppermute x0 -> x3, starting transfers between devices: none -> 7.36 us  [balance_roads(): ppermute(high, 'yz', tuple(((kk, kk ^ rr) for kk in range(count_all))))]
  transfers between devices with their start and end apart: 3 -> 5, of which waited for: 3 -> 5; matrix products, arithmetic and copies ran while one was open for 1% -> 1% of each run, Pallas kernels for 0% -> 0%
where the time goes in v1:
time: 250 us; the launch traced here: 249 us
  waiting for transfers between devices  121 us (48%)
  other arithmetic  62.7 us (25%)
  matrix products  20.4 us (8%)
  local copies, waits for them, and re-layouts  18.9 us (8%)
  between operations  15.6 us (6%)
  starting transfers between devices  7.62 us (3%)
  loops' own time  3.19 us (1%)
    ppermute x3, waiting for transfers between devices, balance_roads(): ppermute(high, 'yz', tuple(((kk, kk ^ rr) for kk in range(count_all))))  90.2 us
    another operation x7, other arithmetic, local(): lower = jnp.linalg.cholesky(gram)  34.7 us
    another operation x4, other arithmetic, local(): lax.linalg.triangular_solve(lower, sketch, left_side=False, lower=True, t...  19.8 us
    psum x1, waiting for transfers between devices, local(): lax.psum(jnp.dot(sketch.T, sketch, precision=lax.Precision.HIGHEST, prefe...  18.9 us
    reduce_scatter x1, waiting for transfers between devices, local(): lax.psum_scatter(lax.dot_general(basis_half, flat, (((0,), (0,)), ((), ()...  12 us
    dot_general x1, matrix products, local(): lax.dot_general(basis_half, flat, (((0,), (0,)), ((), ())), preferred_ele...  8.3 us
    ppermute x3, starting transfers between devices, balance_roads(): ppermute(high, 'yz', tuple(((kk, kk ^ rr) for kk in range(count_all))))  7.36 us
    dynamic_slice x4, local copies, waits for them, and re-layouts, add_block(): rows = lax.dynamic_slice_in_dim(field, index * block, block, 1)  6.93 us
  transfers between devices with their start and end apart: 5, of which 5 were waited for; matrix products, arithmetic and copies ran while one was open for 1% of the time, Pallas kernels for 0%

profile of v1, /device:TPU:0, one launch (start us, length us, event | category | flops | bytes accessed | tf_op | source)
XLA Modules:
  0.0 249.4 jit_solution(11131254630655246790)
XLA Ops:
  12.8 20.5 %while.13 = (s32[]{:T(128)}, f32[1024,256]{1,0:T(8,128)S(1)}, s32[4]{0:T(128)S(1)}, bf16[1024,32,128]{2,1,0:T(8,128)(2,1)}, f32[32,256]{1,0:T(8,128)S(1)}, /*ind...) while((s32[]{:T(128)}, f32[1024,256]{1,0:T(8,128)S(1)}, ...), condition=%wide.region_2.3_spmd.clone, body=%wide.region_0.2_spmd.clone.sunk | while | flops 542146560 | bytes 10513617 | solution.py:46
  14.1 1.7 constant_dynamic-slice_fusion.8
  15.9 1.7 multiply_reduce_fusion.2
  19.3 1.7 constant_dynamic-slice_fusion.8
  21.0 1.7 multiply_reduce_fusion.2
  24.4 1.7 constant_dynamic-slice_fusion.8
  26.1 1.7 multiply_reduce_fusion.2
  29.5 1.7 constant_dynamic-slice_fusion.8
  33.3 3.0 %collective-permute-start = (f32[1024,256]{1,0:T(8,128)S(1)}, f32[1024,256]{1,0:T(8,128)S(1)}, u32[]{:S(2)}, u32[]{:S(2)}) collective-permute-start(f32[1024,256]{1,0:T(8,128)S(1)} %get-tuple-element.34), channel_id=1, source_target_pairs={{0,2},{2,0},{4,6},{6,4},{8,10},{10,8},{12,14},{14,12},{1,3},{3,1},... | collective-permute-start | bytes 3145736 | tf_op jit(solution)/shard_map/ppermute | solution.py:29
  36.3 23.2 %collective-permute-done = f32[1024,256]{1,0:T(8,128)S(1)} collective-permute-done((f32[1024,256]{1,0:T(8,128)S(1)}, f32[1024,256]{1,0:T(8,128)S(1)}, u32[]{:S(2)}, u32[]{:S(2)}) %collective-permute-start) | collective-permute-done | bytes 1048608 | tf_op jit(solution)/shard_map/ppermute | solution.py:29
  59.6 1.8 collective-permute-start.1
  61.5 22.6 %collective-permute-done.1 = f32[1024,256]{1,0:T(8,128)S(1)} collective-permute-done((f32[1024,256]{1,0:T(8,128)S(1)}, f32[1024,256]{1,0:T(8,128)S(1)}, u32[]{:S(2)}, u32[]{:S(2)}) %collective-permute-start.1) | collective-permute-done | bytes 1048608 | tf_op jit(solution)/shard_map/ppermute | solution.py:29
  84.2 2.5 %collective-permute-start.2 = (f32[1024,256]{1,0:T(8,128)S(1)}, f32[1024,256]{1,0:T(8,128)S(1)}, u32[]{:S(2)}, u32[]{:S(2)}) collective-permute-start(f32[1024,256]{1,0:T(8,128)S(1)} %add.273), channel_id=1, source_target_pairs={{0,8},{2,10},{4,12},{6,14},{8,0},{10,2},{12,4},{14,6},{1,9},{3,11}... | collective-permute-start | bytes 3145736 | tf_op jit(solution)/shard_map/ppermute | solution.py:29
  86.7 44.4 %collective-permute-done.2 = f32[1024,256]{1,0:T(8,128)S(1)} collective-permute-done((f32[1024,256]{1,0:T(8,128)S(1)}, f32[1024,256]{1,0:T(8,128)S(1)}, u32[]{:S(2)}, u32[]{:S(2)}) %collective-permute-start.2) | collective-permute-done | bytes 1048608 | tf_op jit(solution)/shard_map/ppermute | solution.py:29
  131.3 2.5 %fusion.55 = f32[256,256]{0,1:T(8,128)} fusion(f32[1024,256]{1,0:T(8,128)S(1)} %add.274), kind=kOutput, calls=%fused_computation.99 | convolution fusion | flops 805306368 | bytes 1310720 | tf_op jit(solution)/shard_map/dot_general | solution.py:53
  134.0 18.9 %all-reduce.3.cloned.1.call-done = f32[256,256]{0,1:T(8,128)} async-done(((f32[256,256]{0,1:T(8,128)}), f32[256,256]{0,1:T(8,128)}) %all-reduce.3.cloned.1.call-update) | async-done | bytes 262160 | tf_op jit(solution)/shard_map/psum | solution.py:52
  155.0 11.7 %cholesky.50 = f32[128,128]{1,0:T(8,128)S(1)} custom-call(f32[128,128]{1,0:T(8,128)S(1)} %cholesky.118), custom_call_target="Cholesky" | custom-call | tf_op jit(solution)/shard_map/jit(cholesky)/cholesky | solution.py:58
  167.4 9.8 %custom-call.14 = f32[1,128,128]{1,2,0:T(8,128)S(1)} custom-call(f32[1,128,128]{2,1,0:T(8,128)S(1)} %get-tuple-element.121), custom_call_target="InvertDiagBlocksLowerTriangular" | custom-call | tf_op jit(solution)/shard_map/jit(cholesky)/cholesky | solution.py:58
  177.7 11.7 %cholesky.105 = f32[128,128]{1,0:T(8,128)S(1)} custom-call(f32[128,128]{1,0:T(8,128)S(1)} %convolution_subtract_fusion), custom_call_target="Cholesky" | custom-call | tf_op jit(solution)/shard_map/jit(cholesky)/cholesky | solution.py:58
  191.7 4.3 %while.12 = (s32[]{:T(128)}, f32[256,256]{1,0:T(8,128)S(1)}, s32[2,2]{1,0:T(2,128)S(1)}, f32[2,128,128]{2,1,0:T(8,128)S(1)}, s32[]{:T(128)}) while((s32[]{:T(128)}, f32[256,256]{1,0:T(8,128)S(1)}, s32[2,2]{1,0:T(2,128)S(1)}, f32[2,128,128]{2,1,0:T(8,128)S(1)}, s32[]{:T(128)}) %tuple.57), condition=%wide.while_cond, body=%wide.while_body.sunk | while | flops 2 | bytes 131189 | solution.py:59
  195.9 19.7 %custom-call.15 = f32[2,128,128]{1,2,0:T(8,128)S(1)} custom-call(f32[2,128,128]{2,1,0:T(8,128)S(1)} %get-tuple-element.42), custom_call_target="InvertDiagBlocksLowerTriangular" | custom-call | tf_op jit(solution)/shard_map/triangular_solve | solution.py:59
  217.9 8.3 %fusion.29 = f32[256,4096]{1,0:T(8,128)} fusion(bf16[128,8,32,128]{3,2,1,0:T(8,128)(2,1)} %bitcast.53, f32[1024,128]{0,1:T(8,128)S(1)} %fusion.32, f32[1024,128]{0,1:T(8,128)S(1)} %fusion.33), kind=kOutput, calls=%fused_computation.38 | convolution fusion | flops 2148532224 | bytes 13631488 | tf_op jit(solution)/shard_map/dot_general | solution.py:66
  227.6 12.0 %reduce-scatter.2.cloned.1.call-done = f32[128,4096]{1,0:T(8,128)} async-done(((f32[256,4096]{1,0:T(8,128)}), f32[128,4096]{1,0:T(8,128)}) %reduce-scatter.2.cloned.1.call-update) | async-done | bytes 2097168 | tf_op jit(solution)/shard_map/reduce_scatter | solution.py:65
  239.6 1.8 convert_bitcast_fusion
  (54 shorter events, 24.7 us)
Async XLA Ops:
  7.2 145.8 %all-reduce.3.cloned.1.call-start = ((), (), s32[]{:S(2)}) async-start(), calls=%async_computation.1 | async-start | bytes 524288 | tf_op jit(solution)/shard_map/psum | solution.py:52
  33.3 26.2 %collective-permute-start = (f32[1024,256]{1,0:T(8,128)S(1)}, f32[1024,256]{1,0:T(8,128)S(1)}, u32[]{:S(2)}, u32[]{:S(2)}) collective-permute-start(f32[1024,256]{1,0:T(8,128)S(1)} %get-tuple-element.34), channel_id=1, source_target_pairs={{0,2},{2,0},{4,6},{6,4},{8,10},{10,8},{12,14},{14,12},{1,3},{3,1},... | collective-permute-start | bytes 3145736 | tf_op jit(solution)/shard_map/ppermute | solution.py:29
  59.6 24.4 %collective-permute-start.1 = (f32[1024,256]{1,0:T(8,128)S(1)}, f32[1024,256]{1,0:T(8,128)S(1)}, u32[]{:S(2)}, u32[]{:S(2)}) collective-permute-start(f32[1024,256]{1,0:T(8,128)S(1)} %add.272), channel_id=1, source_target_pairs={{0,4},{2,6},{4,0},{6,2},{8,12},{10,14},{12,8},{14,10},{1,5},{3,7},... | collective-permute-start | bytes 3145736 | tf_op jit(solution)/shard_map/ppermute | solution.py:29
  84.2 46.9 %collective-permute-start.2 = (f32[1024,256]{1,0:T(8,128)S(1)}, f32[1024,256]{1,0:T(8,128)S(1)}, u32[]{:S(2)}, u32[]{:S(2)}) collective-permute-start(f32[1024,256]{1,0:T(8,128)S(1)} %add.273), channel_id=1, source_target_pairs={{0,8},{2,10},{4,12},{6,14},{8,0},{10,2},{12,4},{14,6},{1,9},{3,11}... | collective-permute-start | bytes 3145736 | tf_op jit(solution)/shard_map/ppermute | solution.py:29
  133.8 105.8 %reduce-scatter.2.cloned.1.call-start = ((), (), s32[]{:S(2)}) async-start(), calls=%async_computation.2 | async-start | bytes 6291456 | tf_op jit(solution)/shard_map/reduce_scatter | solution.py:65
Sparse Core Ops, SparseCore 0:
  133.9 18.9 all-reduce.2
  226.3 13.2 reduce-scatter.1
